TPU v7x, 32 devices: a whole 2x2x4 slice. The times are simulated.
32 devices in a mesh: shard: 4 (over y, core), ctx: 2 (over x), tp: 4 (over z).
Axes of the slice: x: 2, y: 2, z: 4, core: 2. Of those that a mesh axis runs over, the one named last changes fastest.
Arguments:
- tokens: bfloat16 [4, 1500, 768], P('shard', 'ctx'), may hold values from -8 to 8
- w_qkv: bfloat16 [768, 3, 768], P('shard', None, 'tp'), may hold values from -2 to 2
- b_qv: bfloat16 [2, 768], P(None, ('tp', 'shard')), may hold values from -3 to 3
- w_out: bfloat16 [768, 768], P('tp', 'shard'), may hold values from -1.5 to 1.5
- b_out: bfloat16 [768], P('shard'), may hold values from -2 to 2
- w_fc1: bfloat16 [768, 3072], P('shard', 'tp'), may hold values from -0.21875 to 0.21875
- b_fc1: bfloat16 [3072], P(('tp', 'shard')), may hold values from -3 to 3
- w_fc2: bfloat16 [3072, 768], P('tp', 'shard'), may hold values from -0.109375 to 0.109375
- b_fc2: bfloat16 [768], P('shard'), may hold values from -2 to 2
- ln1_gain: bfloat16 [768], P('shard'), may hold values from 0.25 to 1.75
- ln1_bias: bfloat16 [768], P('shard'), may hold values from -2 to 2
- ln2_gain: bfloat16 [768], P('shard'), may hold values from 0.25 to 1.75
- ln2_bias: bfloat16 [768], P('shard'), may hold values from -2 to 2
- cotangent: bfloat16 [4, 1500, 768], P('shard', 'ctx'), may hold values from -6 to 6
Outputs:
- output: bfloat16 [4, 1500, 768], P('shard', 'ctx')
- grad_tokens: bfloat16 [4, 1500, 768], P('shard', 'ctx')
- grad_w_qkv: float32 [768, 3, 768], P('shard', None, 'tp')
- grad_b_qv: float32 [2, 768], P(None, ('tp', 'shard'))
- grad_w_out: float32 [768, 768], P('tp', 'shard')
- grad_b_out: float32 [768], P('shard')
- grad_w_fc1: float32 [768, 3072], P('shard', 'tp')
- grad_b_fc1: float32 [3072], P(('tp', 'shard'))
- grad_w_fc2: float32 [3072, 768], P('tp', 'shard')
- grad_b_fc2: float32 [768], P('shard')
- grad_ln1_gain: float32 [768], P('shard')
- grad_ln1_bias: float32 [768], P('shard')
- grad_ln2_gain: float32 [768], P('shard')
- grad_ln2_bias: float32 [768], P('shard')
All inputs are finite; a program needn't handle non-finite values.
Results may differ from a plain program's by a relative error of at most 0.024.
Values may be sent and summed in bfloat16 or wider, within the bound.
No kernel may reach another device: no remote copies, remote signals or barrier semaphores. Data moves between devices by JAX's collectives and lax.ppermute only.
A program may use at most 128 MiB of HBM per device.

v0:
```python
import jax
import jax.numpy as jnp
from jax import lax
from jax.sharding import PartitionSpec as P

HEAD_DIM = 64


def norm_rows(rows, gain_vec, bias_vec):
    row_mean = jnp.mean(rows, axis=-1, keepdims=True)
    centred = rows - row_mean
    variance = jnp.mean(centred * centred, axis=-1, keepdims=True)
    return centred * lax.rsqrt(variance + 1e-05) * gain_vec + bias_vec


def exact_gelu(rows):
    return jax.nn.gelu(rows, approximate=False)


def split_heads(tensor):
    return tensor.reshape(
        tensor.shape[0], tensor.shape[1], tensor.shape[2] // HEAD_DIM, HEAD_DIM
    ).transpose(2, 0, 1, 3)


def join_heads(tensor):
    return tensor.transpose(1, 2, 0, 3).reshape(
        tensor.shape[1], tensor.shape[2], tensor.shape[0] * tensor.shape[3]
    )


def tensor_sum(partial_rows):
    return lax.psum(partial_rows.astype(jnp.bfloat16), "tp").astype(jnp.float32)


def head_forward(operands):
    queries, all_keys, values = operands
    scores = (
        jnp.einsum("cfd,cgd->cfg", queries, all_keys, preferred_element_type=jnp.float32) * 0.125
    )
    row_max = jnp.max(scores, axis=-1, keepdims=True)
    exponent = jnp.exp(scores - row_max)
    row_total = jnp.sum(exponent, axis=-1, keepdims=True)
    probabilities = (exponent / row_total).astype(jnp.bfloat16)
    head_out = jnp.einsum("cfg,cgd->cfd", probabilities, values, preferred_element_type=jnp.float32)
    return (head_out, (row_max + jnp.log(row_total))[..., 0])


def head_backward(operands):
    queries, all_keys, values, grad_out, logsum = operands
    scores = (
        jnp.einsum("cfd,cgd->cfg", queries, all_keys, preferred_element_type=jnp.float32) * 0.125
    )
    probabilities = jnp.exp(scores - logsum[..., None])
    grad_values = jnp.einsum(
        "cfg,cfd->cgd",
        probabilities.astype(jnp.bfloat16),
        grad_out,
        preferred_element_type=jnp.float32,
    )
    grad_probs = jnp.einsum("cfd,cgd->cfg", grad_out, values, preferred_element_type=jnp.float32)
    row_delta = jnp.sum(probabilities * grad_probs, axis=-1, keepdims=True)
    grad_scores = (probabilities * (grad_probs - row_delta)).astype(jnp.bfloat16)
    grad_queries = (
        jnp.einsum("cfg,cgd->cfd", grad_scores, all_keys, preferred_element_type=jnp.float32)
        * 0.125
    )
    grad_keys = (
        jnp.einsum("cfg,cfd->cgd", grad_scores, queries, preferred_element_type=jnp.float32) * 0.125
    )
    return (grad_queries, grad_keys, grad_values)


def per_device(
    tokens,
    w_qkv,
    b_qv,
    w_out,
    b_out,
    w_fc1,
    b_fc1,
    w_fc2,
    b_fc2,
    ln1_gain,
    ln1_bias,
    ln2_gain,
    ln2_bias,
    cotangent,
):
    vectors = jnp.stack([ln1_gain, ln1_bias, b_out, ln2_gain, ln2_bias, b_fc2], axis=1)
    qv_columns = b_qv.T
    fc1_columns = b_fc1[:, None]
    gathered = (
        lax.all_gather(w_qkv, "shard", axis=0, tiled=True),
        lax.all_gather(qv_columns, "shard", axis=0, tiled=True),
        lax.all_gather(vectors, "shard", axis=0, tiled=True),
        lax.all_gather(w_out, "shard", axis=1, tiled=True),
        lax.all_gather(w_fc1, "shard", axis=0, tiled=True),
        lax.all_gather(fc1_columns, "shard", axis=0, tiled=True),
        lax.all_gather(w_fc2, "shard", axis=1, tiled=True),
    )
    full_qkv, full_qv, full_vectors, full_out, full_fc1, full_fc1_bias, full_fc2 = gathered
    vector_table = full_vectors.astype(jnp.float32)
    gain_one = vector_table[:, 0]
    bias_one = vector_table[:, 1]
    out_bias = vector_table[:, 2]
    gain_two = vector_table[:, 3]
    bias_two = vector_table[:, 4]
    fc2_bias = vector_table[:, 5]
    inputs = tokens.astype(jnp.float32)
    normed_one = norm_rows(inputs, gain_one, bias_one).astype(jnp.bfloat16)
    projected = jnp.einsum(
        "cfd,dtk->cftk", normed_one, full_qkv, preferred_element_type=jnp.float32
    )
    qv_table = full_qv.astype(jnp.float32)
    bias_table = jnp.stack([qv_table[:, 0], jnp.zeros_like(qv_table[:, 0]), qv_table[:, 1]], axis=0)
    projected = (projected + bias_table).astype(jnp.bfloat16)
    queries = projected[:, :, 0]
    all_keys, all_values = (
        lax.all_gather(projected[:, :, 1], "ctx", axis=1, tiled=True),
        lax.all_gather(projected[:, :, 2], "ctx", axis=1, tiled=True),
    )
    split_queries = split_heads(queries)
    split_keys = split_heads(all_keys)
    split_values = split_heads(all_values)
    heads_out, logsum = lax.map(head_forward, (split_queries, split_keys, split_values))
    attended = join_heads(heads_out).astype(jnp.bfloat16)
    attn_part = jnp.einsum("cfk,kd->cfd", attended, full_out, preferred_element_type=jnp.float32)
    attn_sum = tensor_sum(attn_part)
    middle = inputs + (attn_sum + out_bias)
    normed_two = norm_rows(middle, gain_two, bias_two).astype(jnp.bfloat16)
    hidden_pre = jnp.einsum(
        "cfd,dh->cfh", normed_two, full_fc1, preferred_element_type=jnp.float32
    ) + full_fc1_bias[:, 0].astype(jnp.float32)
    activated = exact_gelu(hidden_pre).astype(jnp.bfloat16)
    mlp_part = jnp.einsum("cfh,hd->cfd", activated, full_fc2, preferred_element_type=jnp.float32)
    mlp_sum = tensor_sum(mlp_part)
    output = (middle + (mlp_sum + fc2_bias)).astype(jnp.bfloat16)
    regathered = (
        lax.all_gather(w_qkv, "shard", axis=0, tiled=True),
        lax.all_gather(w_out, "shard", axis=1, tiled=True),
        lax.all_gather(w_fc1, "shard", axis=0, tiled=True),
        lax.all_gather(w_fc2, "shard", axis=1, tiled=True),
    )
    full_qkv, full_out, full_fc1, full_fc2 = regathered
    grad_result = cotangent.astype(jnp.float32)
    grad_fc2 = jnp.einsum("cfh,cfd->hd", activated, cotangent, preferred_element_type=jnp.float32)
    grad_act = jnp.einsum("cfd,hd->cfh", cotangent, full_fc2, preferred_element_type=jnp.float32)
    unused_act, gelu_pull = jax.vjp(exact_gelu, hidden_pre)
    grad_pre = gelu_pull(grad_act)[0].astype(jnp.bfloat16)
    grad_fc1 = jnp.einsum("cfd,cfh->dh", normed_two, grad_pre, preferred_element_type=jnp.float32)
    grad_fc1_bias = jnp.sum(grad_pre.astype(jnp.float32), axis=(0, 1))
    grad_two_part = jnp.einsum(
        "cfh,dh->cfd", grad_pre, full_fc1, preferred_element_type=jnp.float32
    )
    grad_fc2_bias = jnp.sum(grad_result, axis=(0, 1))
    grad_normed_two = tensor_sum(grad_two_part)
    unused_two, pull_two = jax.vjp(norm_rows, middle, gain_two, bias_two)
    grad_mid_norm, grad_gain_two, grad_bias_two = pull_two(grad_normed_two)
    grad_middle = grad_result + grad_mid_norm
    grad_branch = grad_middle.astype(jnp.bfloat16)
    grad_out_bias = jnp.sum(grad_branch.astype(jnp.float32), axis=(0, 1))
    grad_out_w = jnp.einsum(
        "cfk,cfd->kd", attended, grad_branch, preferred_element_type=jnp.float32
    )
    grad_attended = jnp.einsum(
        "cfd,kd->cfk", grad_branch, full_out, preferred_element_type=jnp.float32
    ).astype(jnp.bfloat16)
    head_queries, head_keys, head_values = lax.map(
        head_backward, (split_queries, split_keys, split_values, split_heads(grad_attended), logsum)
    )
    grad_keys, grad_values = (
        lax.psum_scatter(
            join_heads(head_keys).astype(jnp.bfloat16), "ctx", scatter_dimension=1, tiled=True
        ).astype(jnp.float32),
        lax.psum_scatter(
            join_heads(head_values).astype(jnp.bfloat16), "ctx", scatter_dimension=1, tiled=True
        ).astype(jnp.float32),
    )
    grad_projected = jnp.stack([join_heads(head_queries), grad_keys, grad_values], axis=2).astype(
        jnp.bfloat16
    )
    grad_slots = jnp.sum(grad_projected.astype(jnp.float32), axis=(0, 1))
    grad_qv_columns = jnp.stack([grad_slots[0], grad_slots[2]], axis=1)
    grad_qkv_w = jnp.einsum(
        "cfd,cftk->dtk", normed_one, grad_projected, preferred_element_type=jnp.float32
    )
    grad_one_part = jnp.einsum(
        "cftk,dtk->cfd", grad_projected, full_qkv, preferred_element_type=jnp.float32
    )
    grad_normed_one = tensor_sum(grad_one_part)
    unused_one, pull_one = jax.vjp(norm_rows, inputs, gain_one, bias_one)
    grad_in_norm, grad_gain_one, grad_bias_one = pull_one(grad_normed_one)
    grad_tokens = (grad_middle + grad_in_norm).astype(jnp.bfloat16)
    grad_vectors = jnp.stack(
        [grad_gain_one, grad_bias_one, grad_out_bias, grad_gain_two, grad_bias_two, grad_fc2_bias],
        axis=1,
    )
    grad_tuple = (
        grad_qkv_w,
        grad_qv_columns,
        grad_vectors,
        grad_out_w,
        grad_fc1,
        grad_fc1_bias[:, None],
        grad_fc2,
    )
    grad_tuple = (
        lax.psum(grad_tuple[0].astype(jnp.bfloat16), "ctx").astype(jnp.float32),
        lax.psum(grad_tuple[1].astype(jnp.bfloat16), "ctx").astype(jnp.float32),
        lax.psum(grad_tuple[2].astype(jnp.bfloat16), "ctx").astype(jnp.float32),
        lax.psum(grad_tuple[3].astype(jnp.bfloat16), "ctx").astype(jnp.float32),
        lax.psum(grad_tuple[4].astype(jnp.bfloat16), "ctx").astype(jnp.float32),
        lax.psum(grad_tuple[5].astype(jnp.bfloat16), "ctx").astype(jnp.float32),
        lax.psum(grad_tuple[6].astype(jnp.bfloat16), "ctx").astype(jnp.float32),
    )
    grad_slices = (
        lax.psum_scatter(
            grad_tuple[0].astype(jnp.bfloat16), "shard", scatter_dimension=0, tiled=True
        ).astype(jnp.float32),
        lax.psum_scatter(
            grad_tuple[1].astype(jnp.bfloat16), "shard", scatter_dimension=0, tiled=True
        ).astype(jnp.float32),
        lax.psum_scatter(
            grad_tuple[2].astype(jnp.bfloat16), "shard", scatter_dimension=0, tiled=True
        ).astype(jnp.float32),
        lax.psum_scatter(
            grad_tuple[3].astype(jnp.bfloat16), "shard", scatter_dimension=1, tiled=True
        ).astype(jnp.float32),
        lax.psum_scatter(
            grad_tuple[4].astype(jnp.bfloat16), "shard", scatter_dimension=0, tiled=True
        ).astype(jnp.float32),
        lax.psum_scatter(
            grad_tuple[5].astype(jnp.bfloat16), "shard", scatter_dimension=0, tiled=True
        ).astype(jnp.float32),
        lax.psum_scatter(
            grad_tuple[6].astype(jnp.bfloat16), "shard", scatter_dimension=1, tiled=True
        ).astype(jnp.float32),
    )
    slice_qkv, slice_qv, slice_vectors, slice_out, slice_fc1, slice_fc1_bias, slice_fc2 = (
        grad_slices
    )
    return (
        output,
        grad_tokens,
        slice_qkv,
        slice_qv.T,
        slice_out,
        slice_vectors[:, 2],
        slice_fc1,
        slice_fc1_bias[:, 0],
        slice_fc2,
        slice_vectors[:, 5],
        slice_vectors[:, 0],
        slice_vectors[:, 1],
        slice_vectors[:, 3],
        slice_vectors[:, 4],
    )


def solution(mesh):
    placed = (
        P("shard", "ctx", None),
        P("shard", None, "tp"),
        P(None, ("tp", "shard")),
        P("tp", "shard"),
        P("shard"),
        P("shard", "tp"),
        P(("tp", "shard")),
        P("tp", "shard"),
        P("shard"),
        P("shard"),
        P("shard"),
        P("shard"),
        P("shard"),
        P("shard", "ctx", None),
    )
    return jax.shard_map(
        per_device,
        mesh=mesh,
        in_specs=placed,
        out_specs=(
            P("shard", "ctx", None),
            P("shard", "ctx", None),
            P("shard", None, "tp"),
            P(None, ("tp", "shard")),
            P("tp", "shard"),
            P("shard"),
            P("shard", "tp"),
            P(("tp", "shard")),
            P("tp", "shard"),
            P("shard"),
            P("shard"),
            P("shard"),
            P("shard"),
            P("shard"),
        ),
        check_vma=False,
    )
```

profile of v0, /device:TPU:0, one launch (start us, length us, event | category | flops | bytes accessed | tf_op | source)
XLA Modules:
  0.0 549.9 jit_solution(6944061020995750979)
XLA Ops:
  12.1 6.2 %all-gather.4 = bf16[4,48,2]{1,2,0:T(2,128)(2,1)S(1)} all-gather(bf16[1,48,2]{1,2,0:T(2,128)(2,1)} %bitcast.239), channel_id=1, replica_groups=mesh['shard'=4,'ctx'=2,'tp'=4] {'shard'}, dimensions={0}, use_global_device_ids=true | all-gather | bytes 960 | tf_op jit(solution)/shard_map/all_gather | solution.py:95
  21.7 5.5 all-gather.3
  28.0 7.1 %all_gather.36 = bf16[192,768]{0,1:T(8,128)(2,1)} all-gather(bf16[192,192]{0,1:T(8,128)(2,1)S(1)} %copy.88), channel_id=1, replica_groups=mesh['shard'=4,'ctx'=2,'tp'=4] {'shard'}, dimensions={1}, use_global_device_ids=true | all-gather | bytes 368640 | tf_op jit(solution)/shard_map/all_gather | solution.py:97
  35.4 13.1 %all_gather.32 = bf16[768,3,192]{2,1,0:T(4,128)(2,1)S(1)} all-gather(bf16[192,3,192]{2,1,0:T(4,128)(2,1)S(1)} %copy.78), channel_id=1, replica_groups=mesh['shard'=4,'ctx'=2,'tp'=4] {'shard'}, dimensions={0}, use_global_device_ids=true | all-gather | bytes 1105920 | tf_op jit(solution)/shard_map/all_gather | solution.py:94
  55.9 20.3 %all-gather.1 = bf16[1,1500,1,192]{3,2,0,1:T(2,128)(2,1)S(1)} all-gather(bf16[1,750,1,192]{3,2,0,1:T(2,128)(2,1)} %copy.84), channel_id=3, replica_groups=mesh['shard'=4,'ctx'=2,'tp'=4] {'ctx'}, dimensions={1}, use_global_device_ids=true | all-gather | bytes 864000 | tf_op jit(solution)/shard_map/all_gather | solution.py:121
  84.4 19.4 %all-gather = bf16[1,1500,1,192]{3,2,0,1:T(2,128)(2,1)S(1)} all-gather(bf16[1,750,1,192]{3,2,0,1:T(2,128)(2,1)} %copy.82), channel_id=2, replica_groups=mesh['shard'=4,'ctx'=2,'tp'=4] {'ctx'}, dimensions={1}, use_global_device_ids=true | all-gather | bytes 864000 | tf_op jit(solution)/shard_map/all_gather | solution.py:120
  109.4 14.3 %while.26 = (s32[]{:T(128)}, bf16[3,1,750,64]{2,3,1,0:T(8,128)(2,1)}, f32[3,1,750]{2,1,0:T(1,128)S(1)}, bf16[3,1,750,64]{3,2,1,0:T(8,128)(2,1)S(1)}, bf16[3,1,15...) while((s32[]{:T(128)}, bf16[3,1,750,64]{2,3,1,0:T(8,128)(2,1)}, ...), condition=%wide.region_5.6_spmd, body=%wide.region_2.5_spmd.sunk | while | flops 298124256 | bytes 17119008 | solution.py:126
  129.2 5.8 %all-reduce = bf16[768]{0:T(1024)(128)(2,1)S(1)} all-reduce(bf16[768]{0:T(1024)(128)(2,1)S(1)} %dynamic-update-slice), channel_id=4, replica_groups=mesh['shard'=4,'ctx'=2,'tp'=4] {'shard'}, use_global_device_ids=true, to_apply=%add | all-reduce | flops 768 | bytes 3072
  135.0 48.6 %all-reduce.13.cloned.1.call-done = bf16[1,750,768]{2,1,0:T(8,128)(2,1)} async-done(((bf16[1,750,768]{2,1,0:T(8,128)(2,1)}), bf16[1,750,768]{2,1,0:T(8,128)(2,1)}) %all-reduce.13.cloned.1.call-update) | async-done | bytes 1152016 | tf_op jit(solution)/shard_map/psum | solution.py:33
  186.1 9.1 %multiply_convert_fusion.1 = (bf16[750,768]{1,0:T(8,128)(2,1)}, f32[750,768]{1,0:T(8,128)}, f32[750,768]{1,0:T(8,128)}) fusion(f32[768]{0:T(1024)S(1)} %convert_element_type.289, bf16[768,768]{1,0:T(8,128)(2,1)} %all-gather.8.cloned.1.call-done, f32[768]{0:T(1024)S(1)} %get-tuple-element.136, f32[768]{0:T(1024)S(1)} %get-tuple-element.137, ...), kind=kOutput, calls=%fused_computation.83 | convolution fusion | flops 927936000 | bytes 9261936 | tf_op jit(solution)/shard_map/cfd,dh->cfh/dot_general | solution.py:132
  195.3 4.8 fusion.98
  203.3 55.2 %all-reduce.15.cloned.1.call-done = bf16[1,750,768]{2,1,0:T(8,128)(2,1)} async-done(((bf16[1,750,768]{2,1,0:T(8,128)(2,1)}), bf16[1,750,768]{2,1,0:T(8,128)(2,1)}) %all-reduce.15.cloned.1.call-update) | async-done | bytes 1152016 | tf_op jit(solution)/shard_map/psum | solution.py:33
  269.4 25.9 %while.27 = (s32[]{:T(128)}, bf16[3,1,750,64]{2,3,1,0:T(8,128)(2,1)}, bf16[3,1,1500,64]{2,3,1,0:T(8,128)(2,1)}, bf16[3,1,1500,64]{2,3,1,0:T(8,128)(2,1)}, bf16[3...) while((s32[]{:T(128)}, ...), condition=%wide.region_15.16_spmd, body=%wide.region_13.15_spmd.sunk | while | flops 729143232 | bytes 49712548 | solution.py:169
  296.7 3.8 fusion.67
  300.5 37.4 %all-reduce.21.cloned.1.call-done = (bf16[1,1500,192]{1,2,0:T(8,128)(2,1)}, bf16[1,1500,192]{1,2,0:T(8,128)(2,1)}) async-done(((bf16[1,1500,192]{1,2,0:T(8,128)(2,1)}, bf16[1,1500,192]{1,2,0:T(8,128)(2,1)}), (bf16[1,1500,192]{1,2,0:T(8,128)(2,1)}, bf16[1,1500,192]{1,2,0:T(8,128)(2,1)})) %all-reduce.21.cloned.1.call-update) | async-done | bytes 1152016
  351.0 3.8 convolution_convert_fusion
  354.9 3.9 convolution_convert_fusion.1
  361.5 75.2 %all-reduce.17.cloned.1.call-done = (bf16[1,750,768]{2,1,0:T(8,128)(2,1)}, bf16[1,750,768]{2,1,0:T(8,128)(2,1)}) async-done(((bf16[1,750,768]{2,1,0:T(8,128)(2,1)}, bf16[1,750,768]{2,1,0:T(8,128)(2,1)}), (bf16[1,750,768]{2,1,0:T(8,128)(2,1)}, bf16[1,750,768]{2,1,0:T(8,128)(2,1)})) %all-reduce.17.cloned.1.call-update) | async-done | bytes 2304016 | tf_op jit(solution)/shard_map/psum | solution.py:33
  445.9 22.6 %reduce-scatter.20.cloned.1.call-done = bf16[192,768]{1,0:T(8,128)(2,1)} async-done(((bf16[768,768]{1,0:T(8,128)(2,1)}), bf16[192,768]{1,0:T(8,128)(2,1)}) %reduce-scatter.20.cloned.1.call-update) | async-done | bytes 294928 | tf_op jit(solution)/shard_map/reduce_scatter | solution.py:230
  468.5 28.0 %reduce-scatter.18.cloned.1.call-done = bf16[192,3,192]{2,0,1:T(8,128)(2,1)} async-done(((bf16[768,3,192]{2,0,1:T(8,128)(2,1)}), bf16[192,3,192]{2,0,1:T(8,128)(2,1)}) %reduce-scatter.18.cloned.1.call-update) | async-done | bytes 221200 | tf_op jit(solution)/shard_map/reduce_scatter | solution.py:218
  496.6 4.8 add_convert_fusion
  501.4 17.9 %reduce-scatter.28.cloned.1.call-done = bf16[192,6]{1,0:T(8,128)(2,1)} async-done(((bf16[768,6]{1,0:T(8,128)(2,1)}), bf16[192,6]{1,0:T(8,128)(2,1)}) %reduce-scatter.28.cloned.1.call-update) | async-done | bytes 2320
  520.1 5.1 all-reduce.4
  526.9 8.6 %all-reduce.19.cloned.1.call-done = (bf16[192,3,192]{2,0,1:T(8,128)(2,1)}, bf16[192,192]{1,0:T(8,128)(2,1)}, bf16[192,768]{1,0:T(8,128)(2,1)}, bf16[768,192]{0,1:T(8,128)(2,1)}) async-done(((bf16[192,3,192]{2,0,1:T(8,128)(2,1)}, bf16[192,192]{1,0:T(8,128)(2,1)}, bf16[192,768]{1,0:T(8,128)(2,1)}, bf16[768,192]{0,1:T(8,128)(2,1)}), (bf16[192,3,192]{2,0,1:T(8,128)(2,1)}, bf16[192,192]{1,0:T(8,128)(2,1)}, ...) | async-done | bytes 884752 | tf_op jit(solution)/shard_map/psum | solution.py:209
  (271 shorter events, 126.1 us)
Async XLA Ops:
  8.0 19.9 %copy-start.27 = (bf16[192,192]{1,0:T(8,128)(2,1)S(1)}, bf16[192,192]{1,0:T(8,128)(2,1)}, u32[]{:S(2)}) copy-start(bf16[192,192]{1,0:T(8,128)(2,1)} %param.21) | copy-start | bytes 221188
  8.0 27.1 %copy-start.22 = (bf16[192,3,192]{2,0,1:T(8,128)(2,1)S(1)}, bf16[192,3,192]{2,0,1:T(8,128)(2,1)}, u32[]{:S(2)}) copy-start(bf16[192,3,192]{2,0,1:T(8,128)(2,1)} %param.19) | copy-start | bytes 663556
  8.0 175.6 %all-reduce.13.cloned.1.call-start = ((), (), s32[]{:S(2)}) async-start(), calls=%async_computation.7 | async-start | bytes 2310144 | tf_op jit(solution)/shard_map/psum | solution.py:33
  27.9 158.2 %copy-start.31 = (f32[768]{0:T(1024)}, f32[768]{0:T(1024)S(1)}, u32[]{:S(2)}) copy-start(f32[768]{0:T(1024)S(1)} %get-tuple-element.136) | copy-start | bytes 9220
  35.4 15.3 %copy-start = (bf16[1,750,768]{2,1,0:T(8,128)(2,1)S(1)}, bf16[1,750,768]{2,1,0:T(8,128)(2,1)}, u32[]{:S(2)}) copy-start(bf16[1,750,768]{2,1,0:T(8,128)(2,1)} %param.18) | copy-start | bytes 3456004
  109.4 14.3 %copy-start.9 = (bf16[192,768]{0,1:T(8,128)(2,1)S(1)}, bf16[192,768]{0,1:T(8,128)(2,1)}, u32[]{:S(2)}) copy-start(bf16[192,768]{0,1:T(8,128)(2,1)} %all_gather.36) | copy-start | bytes 884740
  126.4 59.7 %all-gather.8.cloned.1.call-start = ((), (), s32[]{:S(2)}) async-start(), calls=%async_computation.8 | async-start | bytes 1474560 | tf_op jit(solution)/shard_map/all_gather | solution.py:98
  127.0 68.2 %all-gather.10.cloned.1.call-start = ((), (), s32[]{:S(2)}) async-start(), calls=%async_computation.9 | async-start | bytes 1474560 | tf_op jit(solution)/shard_map/all_gather | solution.py:100
  127.6 130.9 %all-reduce.15.cloned.1.call-start = ((), (), s32[]{:S(2)}) async-start(), calls=%async_computation.10 | async-start | bytes 2310144 | tf_op jit(solution)/shard_map/psum | solution.py:33
  203.2 134.7 %all-reduce.21.cloned.1.call-start = ((), (), s32[]{:S(2)}) async-start(), calls=%async_computation.20 | async-start | bytes 2359296
  269.4 26.0 %copy-start.35 = (u32[32]{0:T(128)S(1)}, u32[32]{0:T(128)}, u32[]{:S(2)}) copy-start(u32[32]{0:T(128)} %constant.141) | copy-start | bytes 388
  295.4 141.3 %all-reduce.17.cloned.1.call-start = ((), (), s32[]{:S(2)}) async-start(), calls=%async_computation.18 | async-start | bytes 4620288 | tf_op jit(solution)/shard_map/psum | solution.py:33
  296.7 44.3 %copy-start.15 = (bf16[3,1,750,64]{2,3,1,0:T(8,128)(2,1)S(1)}, bf16[3,1,750,64]{2,3,1,0:T(8,128)(2,1)}, u32[]{:S(2)}) copy-start(bf16[3,1,750,64]{2,3,1,0:T(8,128)(2,1)} %get-tuple-element.98) | copy-start | bytes 864004
  296.7 44.3 %copy-start.17 = (bf16[768,3,192]{0,2,1:T(8,128)(2,1)S(1)}, bf16[768,3,192]{0,2,1:T(8,128)(2,1)}, u32[]{:S(2)}) copy-start(bf16[768,3,192]{0,2,1:T(8,128)(2,1)} %copy.79) | copy-start | bytes 2654212
  343.2 99.4 %reduce-scatter.30.cloned.1.call-start = ((), (), s32[]{:S(2)}) async-start(), calls=%async_computation.17 | async-start | bytes 245760
  344.1 99.4 %reduce-scatter.26.cloned.1.call-start = ((), (), s32[]{:S(2)}) async-start(), calls=%async_computation.15 | async-start | bytes 491520
  348.4 96.7 %reduce-scatter.24.cloned.1.call-start = ((), (), s32[]{:S(2)}) async-start(), calls=%async_computation.14 | async-start | bytes 61440
  350.8 95.1 %reduce-scatter.22.cloned.1.call-start = ((), (), s32[]{:S(2)}) async-start(), calls=%async_computation.13 | async-start | bytes 1474560 | tf_op jit(solution)/shard_map/reduce_scatter | solution.py:236
  354.9 113.7 %reduce-scatter.20.cloned.1.call-start = ((), (), s32[]{:S(2)}) async-start(), calls=%async_computation.12 | async-start | bytes 1474560 | tf_op jit(solution)/shard_map/reduce_scatter | solution.py:230
  358.8 137.7 %reduce-scatter.18.cloned.1.call-start = ((), (), s32[]{:S(2)}) async-start(), calls=%async_computation.11 | async-start | bytes 1474560 | tf_op jit(solution)/shard_map/reduce_scatter | solution.py:218
  361.4 78.8 %copy-start.29 = (f32[750]{0:T(1024)S(1)}, f32[750]{0:T(1024)}, u32[]{:S(2)}) copy-start(f32[750]{0:T(1024)} %copy-done.28) | copy-start | bytes 9004
  361.4 157.8 %reduce-scatter.28.cloned.1.call-start = ((), (), s32[]{:S(2)}) async-start(), calls=%async_computation.16 | async-start | bytes 245760
  440.2 56.4 %copy-start.30 = (f32[768]{0:T(1024)S(1)}, f32[768]{0:T(1024)}, u32[]{:S(2)}) copy-start(f32[768]{0:T(1024)} %get-tuple-element.135) | copy-start | bytes 9220
  442.5 93.0 %all-reduce.19.cloned.1.call-start = ((), (), s32[]{:S(2)}) async-start(), calls=%async_computation.19 | async-start | bytes 1966080 | tf_op jit(solution)/shard_map/psum | solution.py:209
  (46 other events, 98.1 us)
Sparse Core Ops, SparseCore 0:
  126.6 57.0 all-reduce.12
  203.3 55.1 all-reduce.14
  295.5 42.3 all-reduce.20
  343.3 93.3 all-reduce.16
  496.7 38.7 all-reduce.18
Sparse Core Ops, SparseCore 1:
  128.5 18.6 all-gather.7
  148.6 17.3 all-gather.9
  346.1 19.7 reduce-scatter.29
  369.0 20.7 reduce-scatter.25
  392.8 19.5 reduce-scatter.23
  414.9 25.5 reduce-scatter.21
  442.9 25.5 reduce-scatter.19
  470.9 25.5 reduce-scatter.17
  499.4 19.8 reduce-scatter.27
where the time goes:
time: 552 us; the launch traced here: 550 us
  waiting for transfers between devices  295 us (53%)
  blocking collectives  82.5 us (15%)
  matrix products  67.9 us (12%)
  local copies, waits for them, and re-layouts  51 us (9%)
  other arithmetic  35.2 us (6%)
  between operations  17.4 us (3%)
    psum x3, waiting for transfers between devices, tensor_sum(): return lax.psum(partial_rows.astype(jnp.bfloat16), 'tp').astype(jnp.float32)  179 us
    unnamed x19, waiting for transfers between devices  56.6 us
    reduce_scatter x1, waiting for transfers between devices, per_device(): lax.psum_scatter(grad_tuple[0].astype(jnp.bfloat16), 'shard', scatter_dim...  28 us
    reduce_scatter x1, waiting for transfers between devices, per_device(): lax.psum_scatter(grad_tuple[4].astype(jnp.bfloat16), 'shard', scatter_dim...  22.6 us
    all_gather x1, blocking collectives, per_device(): lax.all_gather(projected[:, :, 2], 'ctx', axis=1, tiled=True)  20.3 us
    all_gather x1, blocking collectives, per_device(): lax.all_gather(projected[:, :, 1], 'ctx', axis=1, tiled=True)  19.4 us
    all_gather x1, blocking collectives, per_device(): lax.all_gather(w_qkv, 'shard', axis=0, tiled=True)  13.1 us
    unnamed x71, local copies, waits for them, and re-layouts  12.7 us
  transfers between devices with their start and end apart: 14, of which 8 were waited for; matrix products, arithmetic and copies ran while one was open for 9% of the time, Pallas kernels for 0%

commit v1 on v0

--- a/solution.py
+++ b/solution.py
@@ -30,7 +30,9 @@
 
 
 def tensor_sum(partial_rows):
-    return lax.psum(partial_rows.astype(jnp.bfloat16), "tp").astype(jnp.float32)
+    return jnp.sum(lax.all_gather(partial_rows.astype(jnp.bfloat16), "tp"), axis=0).astype(
+        jnp.float32
+    )
 
 
 def head_forward(operands):

time: 552 us -> 850 us (1.54)
  waiting for transfers between devices: 295 us -> 576 us
  other arithmetic: 35.2 us -> 45.5 us
    all_gather x0 -> x4, waiting for transfers between devices: none -> 338 us  [tensor_sum(): lax.all_gather(partial_rows.astype(jnp.bfloat16), 'tp')]
    psum x3 -> x0, waiting for transfers between devices: 179 us -> none  [tensor_sum(): return lax.psum(partial_rows.astype(jnp.bfloat16), 'tp').astype(jnp.float32)]
    unnamed x19 -> x20, waiting for transfers between devices: 56.6 us -> 91.4 us
    psum x1, waiting for transfers between devices: 8.6 us -> 40.5 us  [per_device(): lax.psum(grad_tuple[0].astype(jnp.bfloat16), 'ctx').astype(jnp.float32)]
    reduce_scatter x1, waiting for transfers between devices: 0.01 us -> 26.6 us  [per_device(): lax.psum_scatter(grad_tuple[6].astype(jnp.bfloat16), 'shard', scatter_dim...]
    all_gather x1, waiting for transfers between devices: 0.03 us -> 12.6 us  [per_device(): lax.all_gather(w_fc1, 'shard', axis=0, tiled=True)]
    all_gather x1, waiting for transfers between devices: 0.01 us -> 9.95 us  [per_device(): lax.all_gather(w_fc2, 'shard', axis=1, tiled=True)]
  transfers between devices with their start and end apart: 14 -> 15, of which waited for: 8 -> 15; matrix products, arithmetic and copies ran while one was open for 9% -> 7% of each run, Pallas kernels for 0% -> 0%
where the time goes in v1:
time: 850 us; the launch traced here: 842 us
  waiting for transfers between devices  576 us (68%)
  blocking collectives  82.5 us (10%)
  matrix products  69.2 us (8%)
  local copies, waits for them, and re-layouts  50.9 us (6%)
  other arithmetic  45.5 us (5%)
  between operations  16 us (2%)
    all_gather x4, waiting for transfers between devices, tensor_sum(): lax.all_gather(partial_rows.astype(jnp.bfloat16), 'tp')  338 us
    unnamed x20, waiting for transfers between devices  91.4 us
    psum x1, waiting for transfers between devices, per_device(): lax.psum(grad_tuple[0].astype(jnp.bfloat16), 'ctx').astype(jnp.float32)  40.5 us
    reduce_scatter x1, waiting for transfers between devices, per_device(): lax.psum_scatter(grad_tuple[0].astype(jnp.bfloat16), 'shard', scatter_dim...  28.2 us
    reduce_scatter x1, waiting for transfers between devices, per_device(): lax.psum_scatter(grad_tuple[4].astype(jnp.bfloat16), 'shard', scatter_dim...  28.2 us
    reduce_scatter x1, waiting for transfers between devices, per_device(): lax.psum_scatter(grad_tuple[6].astype(jnp.bfloat16), 'shard', scatter_dim...  26.6 us
    all_gather x1, blocking collectives, per_device(): lax.all_gather(projected[:, :, 2], 'ctx', axis=1, tiled=True)  20.3 us
    all_gather x1, blocking collectives, per_device(): lax.all_gather(projected[:, :, 1], 'ctx', axis=1, tiled=True)  19.4 us
  transfers between devices with their start and end apart: 15, of which 15 were waited for; matrix products, arithmetic and copies ran while one was open for 7% of the time, Pallas kernels for 0%

profile of v1, /device:TPU:0, one launch (start us, length us, event | category | flops | bytes accessed | tf_op | source)
XLA Modules:
  0.0 841.5 jit_solution(2383244722688818706)
XLA Ops:
  11.3 6.2 all-gather.8
  27.2 7.1 all_gather.60
  34.5 13.1 %all_gather.56 = bf16[768,3,192]{2,1,0:T(4,128)(2,1)S(1)} all-gather(bf16[192,3,192]{2,1,0:T(4,128)(2,1)S(1)} %copy.78), channel_id=1, replica_groups=mesh['shard'=4,'ctx'=2,'tp'=4] {'shard'}, dimensions={0}, use_global_device_ids=true | all-gather | bytes 1105920 | tf_op jit(solution)/shard_map/all_gather | solution.py:96
  55.1 20.3 %all-gather.1 = bf16[1,1500,1,192]{3,2,0,1:T(2,128)(2,1)S(1)} all-gather(bf16[1,750,1,192]{3,2,0,1:T(2,128)(2,1)} %copy.84), channel_id=3, replica_groups=mesh['shard'=4,'ctx'=2,'tp'=4] {'ctx'}, dimensions={1}, use_global_device_ids=true | all-gather | bytes 864000 | tf_op jit(solution)/shard_map/all_gather | solution.py:123
  83.6 19.4 %all-gather = bf16[1,1500,1,192]{3,2,0,1:T(2,128)(2,1)S(1)} all-gather(bf16[1,750,1,192]{3,2,0,1:T(2,128)(2,1)} %copy.82), channel_id=2, replica_groups=mesh['shard'=4,'ctx'=2,'tp'=4] {'ctx'}, dimensions={1}, use_global_device_ids=true | all-gather | bytes 864000 | tf_op jit(solution)/shard_map/all_gather | solution.py:122
  108.5 14.4 %while.26 = (s32[]{:T(128)}, bf16[3,1,750,64]{2,3,1,0:T(8,128)(2,1)}, f32[3,1,750]{2,1,0:T(1,128)S(1)}, bf16[3,1,750,64]{3,2,1,0:T(8,128)(2,1)S(1)}, bf16[3,1,15...) while((s32[]{:T(128)}, bf16[3,1,750,64]{2,3,1,0:T(8,128)(2,1)}, ...), condition=%wide.region_5.6_spmd, body=%wide.region_2.5_spmd.sunk | while | flops 298124256 | bytes 17119008 | solution.py:128
  128.7 5.9 all-reduce
  134.6 80.3 %all-gather.24.cloned.1.call-done = bf16[4,750,768]{2,1,0:T(8,128)(2,1)} async-done(((bf16[1,750,768]{2,1,0:T(8,128)(2,1)}), bf16[4,750,768]{2,1,0:T(8,128)(2,1)}) %all-gather.24.cloned.1.call-update) | async-done | bytes 4608016 | tf_op jit(solution)/shard_map/all_gather | solution.py:33
  219.8 12.6 %all-gather.20.cloned.1.call-done = bf16[768,768]{1,0:T(8,128)(2,1)} async-done(((bf16[192,768]{1,0:T(8,128)(2,1)}), bf16[768,768]{1,0:T(8,128)(2,1)}) %all-gather.20.cloned.1.call-update) | async-done | bytes 1179664 | tf_op jit(solution)/shard_map/all_gather | solution.py:100
  232.4 9.1 %multiply_convert_fusion.1 = (bf16[750,768]{1,0:T(8,128)(2,1)}, f32[750,768]{1,0:T(8,128)}, f32[750,768]{1,0:T(8,128)}) fusion(f32[768]{0:T(1024)S(1)} %convert_element_type.361, bf16[768,768]{1,0:T(8,128)(2,1)} %all-gather.20.cloned.1.call-done, f32[768]{0:T(1024)S(1)} %get-tuple-element.140, f32[768]{0:T(1024)S(1)} %get-tuple-element.141, ...), kind=kOutput, calls=%fused_computation.86 | convolution fusion | flops 927936000 | bytes 9261936 | tf_op jit(solution)/shard_map/cfd,dh->cfh/dot_general | solution.py:134
  241.4 9.9 %all-gather.22.cloned.1.call-done = bf16[768,768]{0,1:T(8,128)(2,1)} async-done(((bf16[768,192]{0,1:T(8,128)(2,1)}), bf16[768,768]{0,1:T(8,128)(2,1)}) %all-gather.22.cloned.1.call-update) | async-done | bytes 1179664 | tf_op jit(solution)/shard_map/all_gather | solution.py:102
  260.0 87.3 %all-gather.28.cloned.1.call-done = bf16[4,750,768]{2,1,0:T(8,128)(2,1)} async-done(((bf16[1,750,768]{2,1,0:T(8,128)(2,1)}), bf16[4,750,768]{2,1,0:T(8,128)(2,1)}) %all-gather.28.cloned.1.call-update) | async-done | bytes 4608016 | tf_op jit(solution)/shard_map/all_gather | solution.py:33
  361.3 25.9 %while.27 = (s32[]{:T(128)}, bf16[3,1,750,64]{2,3,1,0:T(8,128)(2,1)}, bf16[3,1,1500,64]{2,3,1,0:T(8,128)(2,1)}, bf16[3,1,1500,64]{2,3,1,0:T(8,128)(2,1)}, bf16[3...) while((s32[]{:T(128)}, ...), condition=%wide.region_15.16_spmd, body=%wide.region_13.15_spmd.sunk | while | flops 729143232 | bytes 49712548 | solution.py:171
  400.6 28.2 %all-reduce.11.cloned.1.call-done = (bf16[1,1500,192]{1,2,0:T(8,128)(2,1)}, bf16[1,1500,192]{1,2,0:T(8,128)(2,1)}) async-done(((bf16[1,1500,192]{1,2,0:T(8,128)(2,1)}, bf16[1,1500,192]{1,2,0:T(8,128)(2,1)}), (bf16[1,1500,192]{1,2,0:T(8,128)(2,1)}, bf16[1,1500,192]{1,2,0:T(8,128)(2,1)})) %all-reduce.11.cloned.1.call-update) | async-done | bytes 1152016
  439.3 13.3 %reduce-scatter.26.cloned.1.call-done = bf16[192,192]{1,0:T(8,128)(2,1)} async-done(((bf16[768,192]{1,0:T(8,128)(2,1)}), bf16[192,192]{1,0:T(8,128)(2,1)}) %reduce-scatter.26.cloned.1.call-update) | async-done | bytes 73744
  454.2 26.6 %reduce-scatter.22.cloned.1.call-done = bf16[768,192]{0,1:T(8,128)(2,1)} async-done(((bf16[768,768]{0,1:T(8,128)(2,1)}), bf16[768,192]{0,1:T(8,128)(2,1)}) %reduce-scatter.22.cloned.1.call-update) | async-done | bytes 294928 | tf_op jit(solution)/shard_map/reduce_scatter | solution.py:238
  480.8 28.2 %reduce-scatter.20.cloned.1.call-done = bf16[192,768]{1,0:T(8,128)(2,1)} async-done(((bf16[768,768]{1,0:T(8,128)(2,1)}), bf16[192,768]{1,0:T(8,128)(2,1)}) %reduce-scatter.20.cloned.1.call-update) | async-done | bytes 294928 | tf_op jit(solution)/shard_map/reduce_scatter | solution.py:232
  509.0 28.2 %reduce-scatter.18.cloned.1.call-done = bf16[192,3,192]{2,0,1:T(8,128)(2,1)} async-done(((bf16[768,3,192]{2,0,1:T(8,128)(2,1)}), bf16[192,3,192]{2,0,1:T(8,128)(2,1)}) %reduce-scatter.18.cloned.1.call-update) | async-done | bytes 221200 | tf_op jit(solution)/shard_map/reduce_scatter | solution.py:220
  540.9 18.9 %reduce-scatter.30.cloned.1.call-done = bf16[192,1]{1,0:T(8,128)(2,1)} async-done(((bf16[768,1]{1,0:T(8,128)(2,1)}), bf16[192,1]{1,0:T(8,128)(2,1)}) %reduce-scatter.30.cloned.1.call-update) | async-done | bytes 400
  561.3 87.9 %all-gather.26.cloned.1.call-done = bf16[4,750,768]{2,1,0:T(8,128)(2,1)} async-done(((bf16[1,750,768]{2,1,0:T(8,128)(2,1)}), bf16[4,750,768]{2,1,0:T(8,128)(2,1)}) %all-gather.26.cloned.1.call-update) | async-done | bytes 4608016 | tf_op jit(solution)/shard_map/all_gather | solution.py:33
  653.6 15.9 %reduce-scatter.24.cloned.1.call-done = bf16[48,2]{1,0:T(8,128)(2,1)} async-done(((bf16[192,2]{1,0:T(8,128)(2,1)}), bf16[48,2]{1,0:T(8,128)(2,1)}) %reduce-scatter.24.cloned.1.call-update) | async-done | bytes 208
  670.8 40.5 %all-reduce.9.cloned.1.call-done = (bf16[192,3,192]{2,0,1:T(8,128)(2,1)}, bf16[192,192]{1,0:T(8,128)(2,1)}, bf16[192,768]{1,0:T(8,128)(2,1)}, bf16[768,192]{0,1:T(8,128)(2,1)}) async-done(((bf16[192,3,192]{2,0,1:T(8,128)(2,1)}, bf16[192,192]{1,0:T(8,128)(2,1)}, bf16[192,768]{1,0:T(8,128)(2,1)}, bf16[768,192]{0,1:T(8,128)(2,1)}), (bf16[192,3,192]{2,0,1:T(8,128)(2,1)}, bf16[192,192]{1,0:T(8,128)(2,1)}, ...) | async-done | bytes 884752 | tf_op jit(solution)/shard_map/psum | solution.py:211
  718.3 82.8 %all-gather.30.cloned.1.call-done = bf16[4,750,768]{2,1,0:T(8,128)(2,1)} async-done(((bf16[1,750,768]{2,1,0:T(8,128)(2,1)}), bf16[4,750,768]{2,1,0:T(8,128)(2,1)}) %all-gather.30.cloned.1.call-update) | async-done | bytes 4608016 | tf_op jit(solution)/shard_map/all_gather | solution.py:33
  813.6 13.5 %reduce-scatter.28.cloned.1.call-done = bf16[192,6]{1,0:T(8,128)(2,1)} async-done(((bf16[768,6]{1,0:T(8,128)(2,1)}), bf16[192,6]{1,0:T(8,128)(2,1)}) %reduce-scatter.28.cloned.1.call-update) | async-done | bytes 2320
  (267 shorter events, 170.1 us)
Async XLA Ops:
  7.2 19.9 %copy-start.22 = (bf16[192,192]{1,0:T(8,128)(2,1)S(1)}, bf16[192,192]{1,0:T(8,128)(2,1)}, u32[]{:S(2)}) copy-start(bf16[192,192]{1,0:T(8,128)(2,1)} %param.21) | copy-start | bytes 221188
  7.2 27.1 %copy-start.20 = (bf16[192,3,192]{2,0,1:T(8,128)(2,1)S(1)}, bf16[192,3,192]{2,0,1:T(8,128)(2,1)}, u32[]{:S(2)}) copy-start(bf16[192,3,192]{2,0,1:T(8,128)(2,1)} %param.19) | copy-start | bytes 663556
  7.2 207.7 %all-gather.24.cloned.1.call-start = ((), (), s32[]{:S(2)}) async-start(), calls=%async_computation.12 | async-start | bytes 5775360 | tf_op jit(solution)/shard_map/all_gather | solution.py:33
  34.5 15.3 %copy-start = (bf16[1,750,768]{2,1,0:T(8,128)(2,1)S(1)}, bf16[1,750,768]{2,1,0:T(8,128)(2,1)}, u32[]{:S(2)}) copy-start(bf16[1,750,768]{2,1,0:T(8,128)(2,1)} %param.18) | copy-start | bytes 3456004
  108.5 14.4 %copy-start.9 = (bf16[192,768]{0,1:T(8,128)(2,1)S(1)}, bf16[192,768]{0,1:T(8,128)(2,1)}, u32[]{:S(2)}) copy-start(bf16[192,768]{0,1:T(8,128)(2,1)} %all_gather.60) | copy-start | bytes 884740
  122.9 11.7 %copy-start.3 = (bf16[3,1,750,64]{3,2,1,0:T(8,128)(2,1)}, bf16[3,1,750,64]{3,2,1,0:T(8,128)(2,1)S(1)}, u32[]{:S(2)}) copy-start(bf16[3,1,750,64]{3,2,1,0:T(8,128)(2,1)S(1)} %get-tuple-element.394) | copy-start | bytes 864004
  125.7 106.7 %all-gather.20.cloned.1.call-start = ((), (), s32[]{:S(2)}) async-start(), calls=%async_computation.7 | async-start | bytes 1474560 | tf_op jit(solution)/shard_map/all_gather | solution.py:100
  126.4 125.0 %all-gather.22.cloned.1.call-start = ((), (), s32[]{:S(2)}) async-start(), calls=%async_computation.8 | async-start | bytes 1474560 | tf_op jit(solution)/shard_map/all_gather | solution.py:102
  127.1 220.2 %all-gather.28.cloned.1.call-start = ((), (), s32[]{:S(2)}) async-start(), calls=%async_computation.14 | async-start | bytes 5775360 | tf_op jit(solution)/shard_map/all_gather | solution.py:33
  251.4 5.9 copy-start.28
  259.4 169.4 %all-reduce.11.cloned.1.call-start = ((), (), s32[]{:S(2)}) async-start(), calls=%async_computation.21 | async-start | bytes 2359296
  387.3 65.3 %reduce-scatter.26.cloned.1.call-start = ((), (), s32[]{:S(2)}) async-start(), calls=%async_computation.17 | async-start | bytes 491520
  391.8 89.0 %reduce-scatter.22.cloned.1.call-start = ((), (), s32[]{:S(2)}) async-start(), calls=%async_computation.11 | async-start | bytes 1474560 | tf_op jit(solution)/shard_map/reduce_scatter | solution.py:238
  395.3 113.7 %reduce-scatter.20.cloned.1.call-start = ((), (), s32[]{:S(2)}) async-start(), calls=%async_computation.10 | async-start | bytes 1474560 | tf_op jit(solution)/shard_map/reduce_scatter | solution.py:232
  399.3 31.6 %copy-start.15 = (bf16[3,1,750,64]{2,3,1,0:T(8,128)(2,1)S(1)}, bf16[3,1,750,64]{2,3,1,0:T(8,128)(2,1)}, u32[]{:S(2)}) copy-start(bf16[3,1,750,64]{2,3,1,0:T(8,128)(2,1)} %get-tuple-element.98) | copy-start | bytes 864004
  399.3 137.9 %reduce-scatter.18.cloned.1.call-start = ((), (), s32[]{:S(2)}) async-start(), calls=%async_computation.9 | async-start | bytes 1474560 | tf_op jit(solution)/shard_map/reduce_scatter | solution.py:220
  433.4 126.4 %reduce-scatter.30.cloned.1.call-start = ((), (), s32[]{:S(2)}) async-start(), calls=%async_computation.19 | async-start | bytes 245760
  434.4 214.9 %all-gather.26.cloned.1.call-start = ((), (), s32[]{:S(2)}) async-start(), calls=%async_computation.13 | async-start | bytes 5775360 | tf_op jit(solution)/shard_map/all_gather | solution.py:33
  438.2 231.3 %reduce-scatter.24.cloned.1.call-start = ((), (), s32[]{:S(2)}) async-start(), calls=%async_computation.16 | async-start | bytes 61440
  439.2 272.0 %all-reduce.9.cloned.1.call-start = ((), (), s32[]{:S(2)}) async-start(), calls=%async_computation.20 | async-start | bytes 1966080 | tf_op jit(solution)/shard_map/psum | solution.py:211
  537.2 263.9 %all-gather.30.cloned.1.call-start = ((), (), s32[]{:S(2)}) async-start(), calls=%async_computation.15 | async-start | bytes 5775360 | tf_op jit(solution)/shard_map/all_gather | solution.py:33
  540.7 286.5 %reduce-scatter.28.cloned.1.call-start = ((), (), s32[]{:S(2)}) async-start(), calls=%async_computation.18 | async-start | bytes 245760
  808.8 19.2 %copy-start.26 = (bf16[192,1]{0,1:T(2,128)(2,1)S(1)}, bf16[192,1]{0,1:T(2,128)(2,1)}, u32[]{:S(2)}) copy-start(bf16[192,1]{0,1:T(2,128)(2,1)} %copy.104) | copy-start | bytes 1156
  808.8 19.2 %copy-start.27 = (bf16[48,2]{0,1:T(2,128)(2,1)S(1)}, bf16[48,2]{0,1:T(2,128)(2,1)}, u32[]{:S(2)}) copy-start(bf16[48,2]{0,1:T(2,128)(2,1)} %copy.98) | copy-start | bytes 580
  (42 other events, 75.4 us)
Sparse Core Ops, SparseCore 0:
  125.8 89.0 all-gather.23
  216.5 15.8 all-gather.19
  233.9 17.4 all-gather.21
  259.5 87.7 all-gather.27
  387.4 41.3 all-reduce.10
  431.7 20.8 reduce-scatter.25
  455.1 25.6 reduce-scatter.21
  483.4 25.5 reduce-scatter.19
  511.6 25.5 reduce-scatter.17
  540.0 19.7 reduce-scatter.29
  561.4 87.7 all-gather.25
  651.5 17.9 reduce-scatter.23
  672.5 38.6 all-reduce.8
  713.3 87.7 all-gather.29
  808.9 18.2 reduce-scatter.27
